TPU v7x, 128 devices: a whole 4x4x4 slice. The times are simulated.
128 devices in a mesh: row: 4 (over x), col: 32 (over y, z, core).
Axes of the slice: x: 4, y: 4, z: 4, core: 2. Of those that a mesh axis runs over, the one named last changes fastest.
Arguments:
- ancestor_inverse: float32 [16384, 16384], P('col', 'row'), as said below
- panels: float32 [2, 16384, 512], P(None, ('col', 'row')), may hold values from -0.1875 to 0.1875
- pattern: int32 [2, 128, 2], replicated, may hold values 0 or 1
- diag_inverse: float32 [2, 512, 512], replicated, may hold values from -6 to 6
- link_panel: float32 [512, 512], replicated, may hold values from -0.25 to 0.25
- block_list: int32 [32, 4, 32], P('col', 'row'), may hold values from 0 to 7
- gauge_owner: int32 [32, 4, 32], P('col', 'row'), may hold values from 0 to 31, each once within a row
- gauge_weight: float32 [4, 32, 512], P('row', 'col'), may hold values from -0.25 to 0.25
Outputs:
- y_first: float32 [16384, 512], P(('col', 'row'))
- diag_first: float32 [512, 512], replicated
- y_second: float32 [16384, 512], P(('col', 'row'))
- cross_second: float32 [512, 512], replicated
- diag_second: float32 [512, 512], replicated
- gauge_response: float32 [4, 32, 512], P('row', 'col')
Inputs may be any that keep to these rules, and one draw needn't show every extreme that they name: `ancestor_inverse`: with its columns put in natural order the matrix is symmetric.
All inputs are finite; a program needn't handle non-finite values.
Results may differ from a plain program's by a relative error of at most 0.000092.
Values sent between devices are 32-bit elements; how exact they have to be, the bound alone decides.
No kernel may reach another device: no remote copies, remote signals or barrier semaphores. Data moves between devices by JAX's collectives and lax.ppermute only.
A program may use at most 128 MiB of HBM per device.

v0:
```python
import jax
import jax.numpy as jnp
from jax import lax
from jax.sharding import Mesh, PartitionSpec as P

NIB = 8
IBR = 16
HIGH = lax.Precision.HIGH
COL = ("y", "z", "core")
CHIPS = ("x", "y", "z")


def dot(left, right, left_dim=1, right_dim=0, precision=HIGH):
    return lax.dot_general(
        left,
        right,
        (((left_dim,), (right_dim,)), ((), ())),
        precision=precision,
        preferred_element_type=jnp.float32,
    )


def swap_core(value):
    return lax.ppermute(value, "core", [(0, 1), (1, 0)])


def spread(value, axes, count):
    copies = jnp.broadcast_to(value[None], (count,) + value.shape)
    return lax.all_to_all(copies, axes, 0, 0, tiled=True)


def all_sum(partial):
    rows, width = partial.shape
    core = lax.axis_index("core")
    halves = partial.reshape(2, rows // 2, width)
    mine = lax.dynamic_index_in_dim(halves, core, 0, keepdims=False)
    theirs = lax.dynamic_index_in_dim(halves, 1 - core, 0, keepdims=False)
    half = mine + swap_core(theirs)
    pieces = half.reshape(64, rows // 128, width)
    part = lax.all_to_all(pieces, CHIPS, 0, 0, tiled=True).sum(0)
    whole = spread(part, CHIPS, 64).reshape(rows // 2, width)
    other = swap_core(whole)
    first = core == 0
    return jnp.concatenate([jnp.where(first, whole, other), jnp.where(first, other, whole)], 0)


def local(ancestor, panels, pattern, diag_inverse, link, block_list, gauge_owner, gauge_weight):
    row = lax.axis_index("x")
    col = lax.axis_index("y") * 8 + lax.axis_index("z") * 2 + lax.axis_index("core")
    flags = lax.dynamic_index_in_dim(pattern, col * 4 + row, 1, keepdims=False)
    flags = jnp.repeat(flags.astype(jnp.float32), 256, axis=1)
    masked = panels * flags[:, None, :]
    both = jnp.concatenate([masked[0], masked[1]], axis=1)
    gathered = lax.all_gather(both, COL, axis=0, tiled=True)
    own_rows = spread(both, "x", 4).reshape(512, 1024)
    weights = lax.all_to_all(gauge_weight.reshape(32, IBR), COL, 0, 0, tiled=True)
    owner_match = (gauge_owner[0, 0][None, :] == jnp.arange(32, dtype=jnp.int32)[:, None]).astype(
        jnp.float32
    )
    block_match = (block_list[0, 0][:, None] == jnp.arange(NIB, dtype=jnp.int32)[None, :]).astype(
        jnp.float32
    )
    selector = dot(owner_match, block_match, precision=lax.Precision.HIGHEST)
    combine = (selector[:, :, None] * weights[:, None, :]).reshape(32, NIB * IBR)
    z = dot(ancestor, gathered)
    g_first = dot(own_rows[:, :512], z[:, :512], 0, 0)
    g_cross = dot(z[:, :512], own_rows[:, 512:], 0, 0)
    g_second = dot(own_rows[:, 512:], z[:, 512:], 0, 0)
    z_rows = lax.all_to_all(z.reshape(4, 128, 1024), "x", 0, 0, tiled=True).sum(0)
    grams = all_sum(jnp.concatenate([g_first, g_cross, g_second], 0))
    y_first = -z_rows[:, :512]
    y_second = -(z_rows[:, 512:] + dot(y_first, link))
    shares = dot(combine, y_second)
    gauge = lax.all_to_all(shares, COL, 0, 0, tiled=True).sum(0).reshape(1, 1, 512)
    diag_first = diag_inverse[0] + grams[:512]
    cross = grams[512:1024]
    cross_second = cross - dot(diag_first, link)
    diag_second = (
        diag_inverse[1] + grams[1024:] - dot(cross, link, 0, 0) - dot(link, cross_second, 0, 0)
    )
    return (y_first, diag_first, y_second, cross_second, diag_second, gauge)


def solution(mesh):
    grid = Mesh(mesh.devices.reshape(4, 4, 4, 2), ("x", "y", "z", "core"))
    in_specs = (
        P(COL, "x"),
        P(None, COL + ("x",), None),
        P(),
        P(),
        P(),
        P(COL, "x", None),
        P(COL, "x", None),
        P("x", COL, None),
    )
    out_specs = (P(COL + ("x",), None), P(), P(COL + ("x",), None), P(), P(), P("x", COL, None))
    return jax.shard_map(local, mesh=grid, in_specs=in_specs, out_specs=out_specs, check_vma=False)
```

profile of v0, /device:TPU:1, one launch (start us, length us, event | category | flops | bytes accessed | tf_op | source)
XLA Modules:
  0.0 265.8 jit_solution(2948248204228471022)
XLA Ops:
  7.2 0.9 convert_reduce_fusion
  8.2 0.1 broadcast_bitcast_fusion
  8.2 1.1 broadcast_multiply_fusion
  9.4 0.8 pad_maximum_fusion.2
  10.2 2.6 broadcast_in_dim.7
  12.9 4.8 %all-to-all-start.1 = ((f32[4,128,1024]{2,1,0:T(8,128)}), f32[4,128,1024]{2,1,0:T(8,128)S(1)}, u32[]{:S(2)}, u32[]{:S(2)}) async-start(f32[4,128,1024]{2,1,0:T(8,128)} %broadcast_in_dim.7), calls=%async_computation.1 | async-start | bytes 4194304 | tf_op jit(solution)/shard_map/all_to_all | solution.py:29
  17.7 69.4 %all-gather.2.cloned.1.call-done = f32[4096,1024]{1,0:T(8,128)} async-done(((f32[128,1024]{1,0:T(8,128)}), f32[4096,1024]{1,0:T(8,128)}) %all-gather.2.cloned.1.call-update) | async-done | bytes 16777232 | tf_op jit(solution)/shard_map/all_gather | solution.py:54
  87.1 19.4 %fusion.16 = f32[1024,512]{0,1:T(8,128)} fusion(f32[4096,1024]{1,0:T(8,128)} %all-gather.2.cloned.1.call-done, f32[512,4096]{1,0:T(8,128)} %param.8), kind=kOutput, calls=%fused_computation.38 | convolution fusion | flops 12884901888 | bytes 27262976 | tf_op jit(solution)/shard_map/dot_general | solution.py:14
  106.5 2.3 fusion.3
  108.8 2.3 fusion.8
  111.1 2.3 fusion.5
  113.3 0.3 pad_maximum_fusion
  113.6 1.6 copy-done.1
  115.3 0.1 dynamic-slice_bitcast_fusion
  115.4 0.5 collective-permute-start
  115.9 3.3 %collective-permute-done = f32[768,512]{1,0:T(8,128)} collective-permute-done((f32[768,512]{1,0:T(8,128)S(1)}, f32[768,512]{1,0:T(8,128)}, u32[]{:S(2)}, u32[]{:S(2)}) %collective-permute-start) | collective-permute-done | bytes 1572896 | tf_op jit(solution)/shard_map/ppermute | solution.py:24
  119.2 2.2 bitcast_add_fusion
  121.4 1.5 reshape.52
  122.9 8.3 %all-to-all-start.2 = ((f32[64,12,512]{2,1,0:T(8,128)}), f32[64,12,512]{2,1,0:T(8,128)S(1)}, u32[]{:S(2)}, u32[]{:S(2)}) async-start(f32[64,12,512]{2,1,0:T(8,128)} %reshape.52), calls=%async_computation.2 | async-start | bytes 4194304 | tf_op jit(solution)/shard_map/all_to_all | solution.py:40
  131.2 0.5 broadcast.9
  131.7 0.7 reduce.6
  132.4 0.7 all_to_all.28
  133.1 25.8 %all-to-all-done.2 = f32[64,12,512]{2,1,0:T(8,128)S(1)} async-done(((f32[64,12,512]{2,1,0:T(8,128)}), f32[64,12,512]{2,1,0:T(8,128)S(1)}, u32[]{:S(2)}, u32[]{:S(2)}) %all-to-all-start.2) | async-done | bytes 1572896 | tf_op jit(solution)/shard_map/all_to_all | solution.py:40
  158.9 6.5 %all-to-all-start.4 = ((f32[32,1,16]{2,1,0:T(1,128)}), f32[32,1,16]{2,1,0:T(1,128)S(1)}, u32[]{:S(2)}, u32[]{:S(2)}) async-start(f32[32,1,16]{2,1,0:T(1,128)} %bitcast.13), calls=%async_computation.4 | async-start | bytes 32768 | tf_op jit(solution)/shard_map/all_to_all | solution.py:56
  165.3 0.2 reduce_sum.28
  165.5 6.8 %all-to-all-done.4 = f32[32,1,16]{2,1,0:T(1,128)S(1)} async-done(((f32[32,1,16]{2,1,0:T(1,128)}), f32[32,1,16]{2,1,0:T(1,128)S(1)}, u32[]{:S(2)}, u32[]{:S(2)}) %all-to-all-start.4) | async-done | bytes 2080 | tf_op jit(solution)/shard_map/all_to_all | solution.py:56
  172.3 0.2 broadcast_in_dim.8
  172.6 32.3 %all_to_all.38 = f32[64,12,512]{2,1,0:T(8,128)S(1)} all-to-all(f32[64,12,512]{2,1,0:T(8,128)S(1)} %broadcast_in_dim.8), channel_id=1, replica_groups=mesh['x'=4,'y'=4,'z'=4,'core'=2] {'x','y','z'}, dimensions={0} | all-to-all | bytes 3145728 | tf_op jit(solution)/shard_map/all_to_all | solution.py:29
  204.9 4.4 %all-to-all-start = ((f32[4,128,1024]{2,1,0:T(8,128)}), f32[4,128,1024]{2,1,0:T(8,128)}, u32[]{:S(2)}, u32[]{:S(2)}) async-start(f32[4,128,1024]{2,1,0:T(8,128)} %bitcast.3), calls=%async_computation | async-start | bytes 4194304 | tf_op jit(solution)/shard_map/all_to_all | solution.py:69
  209.3 1.3 reshape.53
  210.7 2.9 %collective-permute-start.1 = (f32[768,512]{1,0:T(8,128)}, f32[768,512]{1,0:T(8,128)}, u32[]{:S(2)}, u32[]{:S(2)}) collective-permute-start(f32[768,512]{1,0:T(8,128)} %reshape.53), channel_id=1, source_target_pairs={{0,1},{1,0},{2,3},{3,2},{4,5},{5,4},{6,7},{7,6},{8,9},{9,8},{10,11... | collective-permute-start | bytes 4718600 | tf_op jit(solution)/shard_map/ppermute | solution.py:24
  213.6 0.2 fusion.12
  213.8 0.1 copy.20
  213.9 19.0 %all-to-all-done = f32[4,128,1024]{2,1,0:T(8,128)} async-done(((f32[4,128,1024]{2,1,0:T(8,128)}), f32[4,128,1024]{2,1,0:T(8,128)}, u32[]{:S(2)}, u32[]{:S(2)}) %all-to-all-start) | async-done | bytes 2097184 | tf_op jit(solution)/shard_map/all_to_all | solution.py:69
  232.9 1.8 reduce_sum.27
  234.7 0.4 fusion
  235.2 0.7 copy-done.7
  235.9 0.2 convolution_bitcast_fusion.1
  236.1 0.7 copy.21
  236.8 7.6 %all-to-all-start.5 = ((f32[32,1,512]{2,1,0:T(1,128)}), f32[32,1,512]{2,1,0:T(1,128)S(1)}, u32[]{:S(2)}, u32[]{:S(2)}) async-start(f32[32,1,512]{2,1,0:T(1,128)} %copy.21), calls=%async_computation.5 | async-start | bytes 131072 | tf_op jit(solution)/shard_map/all_to_all | solution.py:74
  244.4 7.4 %all-to-all-done.5 = f32[32,1,512]{2,1,0:T(1,128)S(1)} async-done(((f32[32,1,512]{2,1,0:T(1,128)}), f32[32,1,512]{2,1,0:T(1,128)S(1)}, u32[]{:S(2)}, u32[]{:S(2)}) %all-to-all-start.5) | async-done | bytes 65568 | tf_op jit(solution)/shard_map/all_to_all | solution.py:74
  251.8 0.6 reduce_sum.29
  252.5 1.9 broadcast_select_fusion
  254.4 0.1 copy-done.5
  254.5 0.2 slice_add_fusion.1
  254.7 1.0 convolution_subtract_fusion
  255.8 1.0 convolution_bitcast_fusion
  256.8 2.2 fusion.2
  (27 shorter events, 0.2 us)
Async XLA Ops:
  7.2 227.5 %copy-start = (f32[512,512]{1,0:T(8,128)S(1)}, f32[512,512]{1,0:T(8,128)}, u32[]{:S(2)}) copy-start(f32[512,512]{1,0:T(8,128)} %param.12) | copy-start | bytes 3145732
  7.2 79.9 %all-gather.2.cloned.1.call-start = ((), (), s32[]{:S(2)}) async-start(), calls=%async_computation.6 | async-start | bytes 17301504 | tf_op jit(solution)/shard_map/all_gather | solution.py:54
  12.9 93.7 %all-to-all-start.1 = ((f32[4,128,1024]{2,1,0:T(8,128)}), f32[4,128,1024]{2,1,0:T(8,128)S(1)}, u32[]{:S(2)}, u32[]{:S(2)}) async-start(f32[4,128,1024]{2,1,0:T(8,128)} %broadcast_in_dim.7), calls=%async_computation.1 | async-start | bytes 4194304 | tf_op jit(solution)/shard_map/all_to_all | solution.py:29
  113.6 1.6 copy-start.1
  115.4 3.8 %collective-permute-start = (f32[768,512]{1,0:T(8,128)S(1)}, f32[768,512]{1,0:T(8,128)}, u32[]{:S(2)}, u32[]{:S(2)}) collective-permute-start(f32[768,512]{1,0:T(8,128)S(1)} %dynamic-slice_bitcast_fusion), channel_id=1, source_target_pairs={{0,1},{1,0},{2,3},{3,2},{4,5},{5,4},{6,7},{7,6},{8,9},{9,8},{10,11... | collective-permute-start | bytes 4718600 | tf_op jit(solution)/shard_map/ppermute | solution.py:24
  122.9 8.8 %copy-start.8 = (f32[1,1,512]{2,1,0:T(1,128)S(1)}, f32[1,1,512]{2,1,0:T(1,128)}, u32[]{:S(2)}) copy-start(f32[1,1,512]{2,1,0:T(1,128)} %param.15) | copy-start | bytes 6148
  122.9 35.9 %all-to-all-start.2 = ((f32[64,12,512]{2,1,0:T(8,128)}), f32[64,12,512]{2,1,0:T(8,128)S(1)}, u32[]{:S(2)}, u32[]{:S(2)}) async-start(f32[64,12,512]{2,1,0:T(8,128)} %reshape.52), calls=%async_computation.2 | async-start | bytes 4194304 | tf_op jit(solution)/shard_map/all_to_all | solution.py:40
  158.9 13.4 %all-to-all-start.4 = ((f32[32,1,16]{2,1,0:T(1,128)}), f32[32,1,16]{2,1,0:T(1,128)S(1)}, u32[]{:S(2)}, u32[]{:S(2)}) async-start(f32[32,1,16]{2,1,0:T(1,128)} %bitcast.13), calls=%async_computation.4 | async-start | bytes 32768 | tf_op jit(solution)/shard_map/all_to_all | solution.py:56
  204.9 28.0 %all-to-all-start = ((f32[4,128,1024]{2,1,0:T(8,128)}), f32[4,128,1024]{2,1,0:T(8,128)}, u32[]{:S(2)}, u32[]{:S(2)}) async-start(f32[4,128,1024]{2,1,0:T(8,128)} %bitcast.3), calls=%async_computation | async-start | bytes 4194304 | tf_op jit(solution)/shard_map/all_to_all | solution.py:69
  209.3 4.3 %copy-start.9 = (s32[1,1,32]{2,1,0:T(1,128)S(1)}, s32[1,1,32]{2,1,0:T(1,128)}, u32[]{:S(2)}) copy-start(s32[1,1,32]{2,1,0:T(1,128)} %param.13) | copy-start | bytes 388
  209.3 4.2 %copy-start.10 = (s32[1,1,32]{2,1,0:T(1,128)S(1)}, s32[1,1,32]{2,1,0:T(1,128)}, u32[]{:S(2)}) copy-start(s32[1,1,32]{2,1,0:T(1,128)} %param.14) | copy-start | bytes 388
  210.7 41.8 %collective-permute-start.1 = (f32[768,512]{1,0:T(8,128)}, f32[768,512]{1,0:T(8,128)}, u32[]{:S(2)}, u32[]{:S(2)}) collective-permute-start(f32[768,512]{1,0:T(8,128)} %reshape.53), channel_id=1, source_target_pairs={{0,1},{1,0},{2,3},{3,2},{4,5},{5,4},{6,7},{7,6},{8,9},{9,8},{10,11... | collective-permute-start | bytes 4718600 | tf_op jit(solution)/shard_map/ppermute | solution.py:24
  234.7 17.8 %copy-start.2 = (f32[768,512]{1,0:T(8,128)S(1)}, f32[768,512]{1,0:T(8,128)}, u32[]{:S(2)}) copy-start(f32[768,512]{1,0:T(8,128)} %reshape.53) | copy-start | bytes 4718596
  234.7 19.7 %copy-start.6 = (f32[128,512]{1,0:T(8,128)}, f32[128,512]{1,0:T(8,128)S(1)}, u32[]{:S(2)}) copy-start(f32[128,512]{1,0:T(8,128)S(1)} %slice_negate_fusion) | copy-start | bytes 786436
  235.2 0.7 copy-start.7
  236.8 15.0 %all-to-all-start.5 = ((f32[32,1,512]{2,1,0:T(1,128)}), f32[32,1,512]{2,1,0:T(1,128)S(1)}, u32[]{:S(2)}, u32[]{:S(2)}) async-start(f32[32,1,512]{2,1,0:T(1,128)} %copy.21), calls=%async_computation.5 | async-start | bytes 131072 | tf_op jit(solution)/shard_map/all_to_all | solution.py:74
  252.5 2.1 copy-start.5
  254.7 1.0 copy-start.3
  255.8 3.2 %copy-start.4 = (f32[512,512]{1,0:T(8,128)}, f32[512,512]{1,0:T(8,128)S(1)}, u32[]{:S(2)}) copy-start(f32[512,512]{1,0:T(8,128)S(1)} %convolution_subtract_fusion) | copy-start | bytes 3145732
Sparse Core Ops, SparseCore 0:
  10.9 76.2 all-gather.1
where the time goes:
time: 267 us; the launch traced here: 266 us
  waiting for transfers between devices  132 us (49%)
  starting transfers between devices  35.1 us (13%)
  blocking collectives  32.3 us (12%)
  matrix products  31.3 us (12%)
  between operations  14.3 us (5%)
  other arithmetic  10.8 us (4%)
  local copies, waits for them, and re-layouts  10.4 us (4%)
    all_gather x1, waiting for transfers between devices, local(): gathered = lax.all_gather(both, COL, axis=0, tiled=True)  69.4 us
    all_to_all x1, blocking collectives, spread(): return lax.all_to_all(copies, axes, 0, 0, tiled=True)  32.3 us
    dot_general x10, matrix products, dot(): lax.dot_general(left, right, (((left_dim,), (right_dim,)), ((), ())), pre...  31.3 us
    all_to_all x1, waiting for transfers between devices, all_sum(): part = lax.all_to_all(pieces, CHIPS, 0, 0, tiled=True).sum(0)  25.8 us
    all_to_all x1, waiting for transfers between devices, local(): lax.all_to_all(z.reshape(4, 128, 1024), 'x', 0, 0, tiled=True).sum(0)  19 us
    all_to_all x1, starting transfers between devices, all_sum(): part = lax.all_to_all(pieces, CHIPS, 0, 0, tiled=True).sum(0)  8.28 us
    all_to_all x1, starting transfers between devices, local(): lax.all_to_all(shares, COL, 0, 0, tiled=True).sum(0).reshape(1, 1, 512)  7.64 us
    all_to_all x1, waiting for transfers between devices, local(): lax.all_to_all(shares, COL, 0, 0, tiled=True).sum(0).reshape(1, 1, 512)  7.36 us
  transfers between devices with their start and end apart: 8, of which 6 were waited for; matrix products, arithmetic and copies ran while one was open for 11% of the time, Pallas kernels for 0%

commit v1 on v0

--- a/solution.py
+++ b/solution.py
@@ -51,7 +51,9 @@
     flags = jnp.repeat(flags.astype(jnp.float32), 256, axis=1)
     masked = panels * flags[:, None, :]
     both = jnp.concatenate([masked[0], masked[1]], axis=1)
-    gathered = lax.all_gather(both, COL, axis=0, tiled=True)
+    gathered = jnp.concatenate(
+        lax.all_to_all(jnp.stack([both] * lax.axis_size(COL)), COL, 0, 0), axis=0
+    )
     own_rows = spread(both, "x", 4).reshape(512, 1024)
     weights = lax.all_to_all(gauge_weight.reshape(32, IBR), COL, 0, 0, tiled=True)
     owner_match = (gauge_owner[0, 0][None, :] == jnp.arange(32, dtype=jnp.int32)[:, None]).astype(

time: 267 us -> 474 us (1.78)
  waiting for transfers between devices: 132 us -> 293 us
  starting transfers between devices: 35.1 us -> 88 us
  between operations: 14.3 us -> 0.93 us
  local copies, waits for them, and re-layouts: 10.4 us -> 17.3 us
    all_to_all x0 -> x1, waiting for transfers between devices: none -> 231 us  [local(): lax.all_to_all(jnp.stack([both] * lax.axis_size(COL)), COL, 0, 0)]
    all_gather x1 -> x0, waiting for transfers between devices: 69.4 us -> none  [local(): gathered = lax.all_gather(both, COL, axis=0, tiled=True)]
    all_to_all x1, starting transfers between devices: 8.28 us -> 42.4 us  [all_sum(): part = lax.all_to_all(pieces, CHIPS, 0, 0, tiled=True).sum(0)]
    ppermute x2, starting transfers between devices: 3.38 us -> 13.3 us  [swap_core(): return lax.ppermute(value, 'core', [(0, 1), (1, 0)])]
    all_to_all x0 -> x1, starting transfers between devices: none -> 9.66 us  [local(): lax.all_to_all(jnp.stack([both] * lax.axis_size(COL)), COL, 0, 0)]
    another operation x0 -> x1, local copies, waits for them, and re-layouts: none -> 7.9 us  [local(): jnp.stack([both] * lax.axis_size(COL))]
  transfers between devices with their start and end apart: 8 -> 8, of which waited for: 6 -> 6; matrix products, arithmetic and copies ran while one was open for 11% -> 6% of each run, Pallas kernels for 0% -> 0%
where the time goes in v1:
time: 474 us; the launch traced here: 473 us
  waiting for transfers between devices  293 us (62%)
  starting transfers between devices  88 us (19%)
  blocking collectives  32.3 us (7%)
  matrix products  31.3 us (7%)
  local copies, waits for them, and re-layouts  17.3 us (4%)
  other arithmetic  10 us (2%)
    all_to_all x1, waiting for transfers between devices, local(): lax.all_to_all(jnp.stack([both] * lax.axis_size(COL)), COL, 0, 0)  231 us
    all_to_all x1, starting transfers between devices, all_sum(): part = lax.all_to_all(pieces, CHIPS, 0, 0, tiled=True).sum(0)  42.4 us
    all_to_all x1, blocking collectives, spread(): return lax.all_to_all(copies, axes, 0, 0, tiled=True)  32.3 us
    dot_general x10, matrix products, dot(): lax.dot_general(left, right, (((left_dim,), (right_dim,)), ((), ())), pre...  31.3 us
    all_to_all x1, waiting for transfers between devices, all_sum(): part = lax.all_to_all(pieces, CHIPS, 0, 0, tiled=True).sum(0)  25.7 us
    all_to_all x1, waiting for transfers between devices, local(): lax.all_to_all(z.reshape(4, 128, 1024), 'x', 0, 0, tiled=True).sum(0)  19 us
    ppermute x2, starting transfers between devices, swap_core(): return lax.ppermute(value, 'core', [(0, 1), (1, 0)])  13.3 us
    all_to_all x1, starting transfers between devices, local(): lax.all_to_all(jnp.stack([both] * lax.axis_size(COL)), COL, 0, 0)  9.66 us
  transfers between devices with their start and end apart: 8, of which 6 were waited for; matrix products, arithmetic and copies ran while one was open for 6% of the time, Pallas kernels for 0%

profile of v1, /device:TPU:1, one launch (start us, length us, event | category | flops | bytes accessed | tf_op | source)
XLA Modules:
  0.0 473.0 jit_solution(3849887678184761845)
XLA Ops:
  0.7 0.9 convert_reduce_fusion
  1.6 0.1 broadcast_bitcast_fusion
  1.7 1.1 broadcast_multiply_fusion
  2.9 7.9 %stack.2 = f32[32,128,1024]{2,1,0:T(8,128)} broadcast(f32[128,1024]{1,0:T(8,128)S(1)} %pad_maximum_fusion.2), dimensions={1,2} | broadcast | bytes 17301504 | tf_op jit(solution)/shard_map/stack | solution.py:55
  10.8 9.7 %all-to-all-start = ((f32[32,128,1024]{2,1,0:T(8,128)}), f32[32,128,1024]{2,1,0:T(8,128)}, u32[]{:S(2)}, u32[]{:S(2)}) async-start(f32[32,128,1024]{2,1,0:T(8,128)} %stack.2), calls=%async_computation | async-start | bytes 33554432 | tf_op jit(solution)/shard_map/all_to_all | solution.py:55
  20.4 231.2 %all-to-all-done = f32[32,128,1024]{2,1,0:T(8,128)} async-done(((f32[32,128,1024]{2,1,0:T(8,128)}), f32[32,128,1024]{2,1,0:T(8,128)}, u32[]{:S(2)}, u32[]{:S(2)}) %all-to-all-start) | async-done | bytes 16777248 | tf_op jit(solution)/shard_map/all_to_all | solution.py:55
  251.6 1.6 broadcast_in_dim.7
  253.2 4.0 all-to-all-start.2
  257.2 19.4 %fusion.16 = f32[1024,512]{0,1:T(8,128)} fusion(f32[4096,1024]{1,0:T(8,128)} %bitcast.2, f32[512,4096]{1,0:T(8,128)} %param.8), kind=kOutput, calls=%fused_computation.38 | convolution fusion | flops 12884901888 | bytes 27262976 | tf_op jit(solution)/shard_map/dot_general | solution.py:14
  276.6 2.2 fusion.5
  278.9 2.3 fusion.8
  281.1 2.3 fusion.3
  283.4 0.3 pad_maximum_fusion
  283.7 1.6 copy-done.1
  285.3 0.1 dynamic-slice_bitcast_fusion
  285.5 10.4 %collective-permute-start = (f32[768,512]{1,0:T(8,128)S(1)}, f32[768,512]{1,0:T(8,128)}, u32[]{:S(2)}, u32[]{:S(2)}) collective-permute-start(f32[768,512]{1,0:T(8,128)S(1)} %dynamic-slice_bitcast_fusion), channel_id=1, source_target_pairs={{0,1},{1,0},{2,3},{3,2},{4,5},{5,4},{6,7},{7,6},{8,9},{9,8},{10,11... | collective-permute-start | bytes 4718600 | tf_op jit(solution)/shard_map/ppermute | solution.py:24
  295.9 3.2 collective-permute-done
  299.0 2.2 bitcast_add_fusion
  301.3 1.5 reshape.58
  302.8 42.4 %all-to-all-start.3 = ((f32[64,12,512]{2,1,0:T(8,128)}), f32[64,12,512]{2,1,0:T(8,128)S(1)}, u32[]{:S(2)}, u32[]{:S(2)}) async-start(f32[64,12,512]{2,1,0:T(8,128)} %reshape.58), calls=%async_computation.3 | async-start | bytes 4194304 | tf_op jit(solution)/shard_map/all_to_all | solution.py:40
  345.2 0.5 broadcast.11
  345.7 0.7 reduce.6
  346.4 0.7 all_to_all.32
  347.1 25.7 %all-to-all-done.3 = f32[64,12,512]{2,1,0:T(8,128)S(1)} async-done(((f32[64,12,512]{2,1,0:T(8,128)}), f32[64,12,512]{2,1,0:T(8,128)S(1)}, u32[]{:S(2)}, u32[]{:S(2)}) %all-to-all-start.3) | async-done | bytes 1572896 | tf_op jit(solution)/shard_map/all_to_all | solution.py:40
  372.8 6.5 %all-to-all-start.5 = ((f32[32,1,16]{2,1,0:T(1,128)}), f32[32,1,16]{2,1,0:T(1,128)S(1)}, u32[]{:S(2)}, u32[]{:S(2)}) async-start(f32[32,1,16]{2,1,0:T(1,128)} %bitcast.14), calls=%async_computation.5 | async-start | bytes 32768 | tf_op jit(solution)/shard_map/all_to_all | solution.py:58
  379.3 0.2 reduce_sum.28
  379.5 6.8 %all-to-all-done.5 = f32[32,1,16]{2,1,0:T(1,128)S(1)} async-done(((f32[32,1,16]{2,1,0:T(1,128)}), f32[32,1,16]{2,1,0:T(1,128)S(1)}, u32[]{:S(2)}, u32[]{:S(2)}) %all-to-all-start.5) | async-done | bytes 2080 | tf_op jit(solution)/shard_map/all_to_all | solution.py:58
  386.3 0.2 broadcast_in_dim.8
  386.5 32.3 %all_to_all.43 = f32[64,12,512]{2,1,0:T(8,128)S(1)} all-to-all(f32[64,12,512]{2,1,0:T(8,128)S(1)} %broadcast_in_dim.8), channel_id=1, replica_groups=mesh['x'=4,'y'=4,'z'=4,'core'=2] {'x','y','z'}, dimensions={0} | all-to-all | bytes 3145728 | tf_op jit(solution)/shard_map/all_to_all | solution.py:29
  418.9 4.5 all-to-all-start.1
  423.3 1.3 reshape.59
  424.7 2.9 collective-permute-start.1
  427.6 0.2 fusion.12
  427.9 19.0 %all-to-all-done.1 = f32[4,128,1024]{2,1,0:T(8,128)} async-done(((f32[4,128,1024]{2,1,0:T(8,128)}), f32[4,128,1024]{2,1,0:T(8,128)}, u32[]{:S(2)}, u32[]{:S(2)}) %all-to-all-start.1) | async-done | bytes 2097184 | tf_op jit(solution)/shard_map/all_to_all | solution.py:71
  446.9 1.8 reduce_sum.27
  448.7 0.4 fusion
  449.2 0.7 copy-done.7
  449.9 0.2 convolution_bitcast_fusion.1
  450.1 0.7 copy.21
  450.8 7.6 %all-to-all-start.6 = ((f32[32,1,512]{2,1,0:T(1,128)}), f32[32,1,512]{2,1,0:T(1,128)S(1)}, u32[]{:S(2)}, u32[]{:S(2)}) async-start(f32[32,1,512]{2,1,0:T(1,128)} %copy.21), calls=%async_computation.6 | async-start | bytes 131072 | tf_op jit(solution)/shard_map/all_to_all | solution.py:76
  458.4 7.4 %all-to-all-done.6 = f32[32,1,512]{2,1,0:T(1,128)S(1)} async-done(((f32[32,1,512]{2,1,0:T(1,128)}), f32[32,1,512]{2,1,0:T(1,128)S(1)}, u32[]{:S(2)}, u32[]{:S(2)}) %all-to-all-start.6) | async-done | bytes 65568 | tf_op jit(solution)/shard_map/all_to_all | solution.py:76
  465.8 0.6 reduce_sum.29
  466.5 1.9 broadcast_select_fusion
  468.4 0.1 copy-done.5
  468.5 0.2 slice_add_fusion.1
  468.7 1.0 convolution_subtract_fusion
  469.8 1.0 convolution_bitcast_fusion
  470.8 2.2 fusion.2
  (27 shorter events, 0.2 us)
Async XLA Ops:
  0.6 448.1 %copy-start = (f32[512,512]{1,0:T(8,128)S(1)}, f32[512,512]{1,0:T(8,128)}, u32[]{:S(2)}) copy-start(f32[512,512]{1,0:T(8,128)} %param.12) | copy-start | bytes 3145732
  10.8 240.8 %all-to-all-start = ((f32[32,128,1024]{2,1,0:T(8,128)}), f32[32,128,1024]{2,1,0:T(8,128)}, u32[]{:S(2)}, u32[]{:S(2)}) async-start(f32[32,128,1024]{2,1,0:T(8,128)} %stack.2), calls=%async_computation | async-start | bytes 33554432 | tf_op jit(solution)/shard_map/all_to_all | solution.py:55
  253.2 23.4 %all-to-all-start.2 = ((f32[4,128,1024]{2,1,0:T(8,128)}), f32[4,128,1024]{2,1,0:T(8,128)S(1)}, u32[]{:S(2)}, u32[]{:S(2)}) async-start(f32[4,128,1024]{2,1,0:T(8,128)} %broadcast_in_dim.7), calls=%async_computation.2 | async-start | bytes 4194304 | tf_op jit(solution)/shard_map/all_to_all | solution.py:29
  283.7 1.6 copy-start.1
  285.5 13.6 %collective-permute-start = (f32[768,512]{1,0:T(8,128)S(1)}, f32[768,512]{1,0:T(8,128)}, u32[]{:S(2)}, u32[]{:S(2)}) collective-permute-start(f32[768,512]{1,0:T(8,128)S(1)} %dynamic-slice_bitcast_fusion), channel_id=1, source_target_pairs={{0,1},{1,0},{2,3},{3,2},{4,5},{5,4},{6,7},{7,6},{8,9},{9,8},{10,11... | collective-permute-start | bytes 4718600 | tf_op jit(solution)/shard_map/ppermute | solution.py:24
  302.8 42.9 %copy-start.8 = (f32[1,1,512]{2,1,0:T(1,128)S(1)}, f32[1,1,512]{2,1,0:T(1,128)}, u32[]{:S(2)}) copy-start(f32[1,1,512]{2,1,0:T(1,128)} %param.15) | copy-start | bytes 6148
  302.8 70.0 %all-to-all-start.3 = ((f32[64,12,512]{2,1,0:T(8,128)}), f32[64,12,512]{2,1,0:T(8,128)S(1)}, u32[]{:S(2)}, u32[]{:S(2)}) async-start(f32[64,12,512]{2,1,0:T(8,128)} %reshape.58), calls=%async_computation.3 | async-start | bytes 4194304 | tf_op jit(solution)/shard_map/all_to_all | solution.py:40
  372.8 13.5 %all-to-all-start.5 = ((f32[32,1,16]{2,1,0:T(1,128)}), f32[32,1,16]{2,1,0:T(1,128)S(1)}, u32[]{:S(2)}, u32[]{:S(2)}) async-start(f32[32,1,16]{2,1,0:T(1,128)} %bitcast.14), calls=%async_computation.5 | async-start | bytes 32768 | tf_op jit(solution)/shard_map/all_to_all | solution.py:58
  418.9 28.0 %all-to-all-start.1 = ((f32[4,128,1024]{2,1,0:T(8,128)}), f32[4,128,1024]{2,1,0:T(8,128)}, u32[]{:S(2)}, u32[]{:S(2)}) async-start(f32[4,128,1024]{2,1,0:T(8,128)} %bitcast.4), calls=%async_computation.1 | async-start | bytes 4194304 | tf_op jit(solution)/shard_map/all_to_all | solution.py:71
  423.3 4.2 copy-start.9
  423.3 4.2 copy-start.10
  424.7 41.8 %collective-permute-start.1 = (f32[768,512]{1,0:T(8,128)}, f32[768,512]{1,0:T(8,128)}, u32[]{:S(2)}, u32[]{:S(2)}) collective-permute-start(f32[768,512]{1,0:T(8,128)} %reshape.59), channel_id=1, source_target_pairs={{0,1},{1,0},{2,3},{3,2},{4,5},{5,4},{6,7},{7,6},{8,9},{9,8},{10,11... | collective-permute-start | bytes 4718600 | tf_op jit(solution)/shard_map/ppermute | solution.py:24
  448.7 17.8 %copy-start.2 = (f32[768,512]{1,0:T(8,128)S(1)}, f32[768,512]{1,0:T(8,128)}, u32[]{:S(2)}) copy-start(f32[768,512]{1,0:T(8,128)} %reshape.59) | copy-start | bytes 4718596
  448.7 19.7 %copy-start.6 = (f32[128,512]{1,0:T(8,128)}, f32[128,512]{1,0:T(8,128)S(1)}, u32[]{:S(2)}) copy-start(f32[128,512]{1,0:T(8,128)S(1)} %slice_negate_fusion) | copy-start | bytes 786436
  449.2 0.7 copy-start.7
  450.8 15.0 %all-to-all-start.6 = ((f32[32,1,512]{2,1,0:T(1,128)}), f32[32,1,512]{2,1,0:T(1,128)S(1)}, u32[]{:S(2)}, u32[]{:S(2)}) async-start(f32[32,1,512]{2,1,0:T(1,128)} %copy.21), calls=%async_computation.6 | async-start | bytes 131072 | tf_op jit(solution)/shard_map/all_to_all | solution.py:76
  466.5 2.1 copy-start.5
  468.7 1.0 copy-start.3
  469.8 3.2 copy-start.4
